TPU v7x, 32 devices: a whole 2x2x4 slice. The times are simulated.
32 devices in a mesh: member: 2 (over x), fsdp: 16 (over z, y, core).
Axes of the slice: x: 2, y: 2, z: 4, core: 2. Of those that a mesh axis runs over, the one named last changes fastest.
Arguments:
- context: bfloat16 [4, 2048, 2048], P(None, 'fsdp', 'member'), may hold values from -6 to 6
- residual: bfloat16 [2048, 2048], P('fsdp', 'member'), may hold values from -6 to 6
- out_weight: bfloat16 [2048, 2048], P('fsdp', 'member'), may hold values from -0.1875 to 0.1875
- in_factor: bfloat16 [4, 2048], P(None, 'member'), may hold values from 0.25 to 1.75
- out_factor: bfloat16 [4, 2048], P(None, 'member'), may hold values from 0.25 to 1.75
- cotangent: bfloat16 [4, 2048, 2048], P(None, 'fsdp', 'member'), may hold values from -0.796875 to 0.796875
Outputs:
- hidden: bfloat16 [4, 2048, 2048], P(None, 'fsdp', 'member')
- grad_context: bfloat16 [4, 2048, 2048], P(None, 'fsdp', 'member')
- grad_weight: float32 [2048, 2048], P('fsdp', 'member')
- grad_in_factor: float32 [4, 2048], P(None, 'member')
- grad_out_factor: float32 [4, 2048], P(None, 'member')
- grad_residual: float32 [2048, 2048], P('fsdp', 'member')
All inputs are finite; a program needn't handle non-finite values.
Results may differ from a plain program's by a relative error of at most 0.013.
Values may be sent and summed in bfloat16 or wider, within the bound.
A program may use at most 64 MiB of HBM per device.

v0:
```python
import jax
import jax.numpy as jnp
from jax import lax
from jax.sharding import PartitionSpec as P


def per_device(context, residual, out_weight, in_factor, out_factor, cotangent):
    in_wide = in_factor.astype(jnp.float32)
    out_wide = out_factor.astype(jnp.float32)
    scaled_local = (context.astype(jnp.float32) * in_wide[:, None, :]).astype(jnp.bfloat16)
    scaled_grad = (cotangent.astype(jnp.float32) * out_wide[:, None, :]).astype(jnp.bfloat16)
    scaled_context = lax.all_gather(scaled_local, "member", axis=2, tiled=True)
    weight = lax.all_gather(out_weight, "fsdp", axis=0, tiled=True)
    projected = jnp.einsum(
        "eti,id->etd", scaled_context, weight, preferred_element_type=jnp.float32
    )
    partial_value = jnp.einsum(
        "etd,id->eti", scaled_grad, weight, preferred_element_type=jnp.float32
    )
    hidden = (residual.astype(jnp.float32)[None] + projected * out_wide[:, None, :]).astype(
        jnp.bfloat16
    )
    backward = lax.psum_scatter(
        partial_value.astype(jnp.bfloat16), "member", scatter_dimension=2, tiled=True
    ).astype(jnp.float32)
    grad_context = (backward * in_wide[:, None, :]).astype(jnp.bfloat16)
    grad_in_local = jnp.sum(context.astype(jnp.float32) * backward, axis=1)
    grad_out_local = jnp.sum(cotangent.astype(jnp.float32) * projected, axis=1)
    grad_in, grad_out = lax.psum((grad_in_local, grad_out_local), "fsdp")
    grad_block = jnp.einsum(
        "eti,etd->id", scaled_context, scaled_grad, preferred_element_type=jnp.float32
    )
    grad_weight = lax.psum_scatter(grad_block, "fsdp", scatter_dimension=0, tiled=True)
    grad_residual = jnp.sum(cotangent.astype(jnp.float32), axis=0)
    return (hidden, grad_context, grad_weight, grad_in, grad_out, grad_residual)


def solution(mesh):
    in_specs = (
        P(None, "fsdp", "member"),
        P("fsdp", "member"),
        P("fsdp", "member"),
        P(None, "member"),
        P(None, "member"),
        P(None, "fsdp", "member"),
    )
    out_specs = (
        P(None, "fsdp", "member"),
        P(None, "fsdp", "member"),
        P("fsdp", "member"),
        P(None, "member"),
        P(None, "member"),
        P("fsdp", "member"),
    )
    return jax.shard_map(
        per_device, mesh=mesh, in_specs=in_specs, out_specs=out_specs, check_vma=False
    )
```

profile of v0, /device:TPU:0, one launch (start us, length us, event | category | flops | bytes accessed | tf_op | source)
XLA Modules:
  0.0 254.6 jit_solution(12831401750798101958)
XLA Ops:
  7.2 0.0 all-gather.5.cloned.1.call-start
  7.2 0.7 all-gather.5.cloned.1.call-update
  7.9 0.0 reduce-scatter.3.cloned.1.call-start
  7.9 0.7 convert_element_type.40
  8.6 54.6 %all-gather.5.cloned.1.call-done = bf16[2048,1024]{1,0:T(8,128)(2,1)} async-done(((bf16[128,1024]{1,0:T(8,128)(2,1)}), bf16[2048,1024]{1,0:T(8,128)(2,1)}) %all-gather.5.cloned.1.call-update) | async-done | bytes 4194320 | tf_op jit(solution)/shard_map/all_gather | solution.py:13
  63.3 6.2 %fusion.4 = bf16[4,128,2048]{2,1,0:T(8,128)(2,1)} fusion(bf16[2048,1024]{1,0:T(8,128)(2,1)} %all-gather.5.cloned.1.call-done, bf16[4,128,1024]{2,1,0:T(8,128)(2,1)} %param.11, f32[4,1024]{1,0:T(4,128)S(1)} %convert_element_type.40), kind=kOutput, calls=%fused_computation.8 | convolution fusion | flops 2150105088 | bytes 7356416 | tf_op jit(solution)/shard_map/etd,id->eti/dot_general | solution.py:17
  69.5 0.0 copy-start.2
  69.5 0.0 copy-start
  69.5 0.0 reduce-scatter.3.cloned.1.call-update
  69.5 0.0 all-gather.3.cloned.1.call-start
  69.6 0.6 copy-done.2
  70.2 0.0 copy-start.4
  70.2 29.9 %reduce-scatter.3.cloned.1.call-done = bf16[4,128,1024]{2,1,0:T(8,128)(2,1)} async-done(((bf16[4,128,2048]{2,1,0:T(8,128)(2,1)}), bf16[4,128,1024]{2,1,0:T(8,128)(2,1)}) %reduce-scatter.3.cloned.1.call-update) | async-done | bytes 1048592 | tf_op jit(solution)/shard_map/reduce_scatter | solution.py:23
  100.1 0.0 copy-done
  100.1 3.2 %fusion.9 = (f32[4,1024]{1,0:T(4,128)S(1)}, bf16[4,128,1024]{2,1,0:T(8,128)(2,1)}, bf16[4,128,1024]{2,1,0:T(8,128)(2,1)}) fusion(bf16[4,128,1024]{2,1,0:T(8,128)(2,1)} %reduce-scatter.3.cloned.1.call-done, bf16[4,128,1024]{2,1,0:T(8,128)(2,1)S(1)} %copy-done, f32[4,1024]{1,0:T(4,128)S(1)} %convert_element_type.38), kind=kLoop, calls=%fused_computation.14 | loop fusion | flops 4190208 | bytes 4227072 | tf_op jit(solution)/shard_map/reduce_sum | solution.py:27
  103.3 0.0 all-gather.3.cloned.1.call-update
  103.3 0.0 reduce-scatter.5.cloned.1.call-start
  103.4 33.2 %all-gather.3.cloned.1.call-done = bf16[4,128,2048]{2,1,0:T(8,128)(2,1)} async-done(((bf16[4,128,1024]{2,1,0:T(8,128)(2,1)}), bf16[4,128,2048]{2,1,0:T(8,128)(2,1)}) %all-gather.3.cloned.1.call-update) | async-done | bytes 2097168 | tf_op jit(solution)/shard_map/all_gather | solution.py:12
  136.6 0.0 copy-done.4
  136.6 7.2 %convolution_bitcast_fusion = f32[2048,1024]{1,0:T(8,128)} fusion(bf16[4,128,2048]{2,1,0:T(8,128)(2,1)} %all-gather.3.cloned.1.call-done, bf16[4,128,1024]{2,1,0:T(8,128)(2,1)S(1)} %copy-done.4, f32[4,1024]{1,0:T(4,128)S(1)} %convert_element_type.40), kind=kOutput, calls=%fused_computation | convolution fusion | flops 2149056512 | bytes 11550720 | tf_op jit(solution)/shard_map/eti,etd->id/dot_general | solution.py:30
  143.8 0.0 copy-start.1
  143.8 0.0 copy-start.3
  143.8 0.0 reduce-scatter.5.cloned.1.call-update
  143.8 0.9 copy-done.1
  144.8 0.7 copy-done.3
  145.5 6.6 %convert_reduce_fusion = (f32[128,1024]{1,0:T(8,128)}, f32[4,1024]{1,0:T(4,128)S(1)}, bf16[4,128,1024]{2,1,0:T(8,128)(2,1)}) fusion(bf16[4,128,1024]{2,1,0:T(8,128)(2,1)S(1)} %copy-done.4, f32[4,1024]{1,0:T(4,128)S(1)} %convert_element_type.40, f32[128,1024]{1,0:T(8,128)S(1)} %convert_element_type.36, bf16[4,128,2048]{2,1,0:T(8,128)(2,1)S(1)} %copy-done.3, ...), kind=kOutput, calls=%fused_computation.5 | convolution fusion | flops 2151018496 | bytes 9469952 | tf_op jit(solution)/shard_map/eti,id->etd/dot_general | solution.py:14
  152.1 64.4 %all-reduce = (f32[4,1024]{1,0:T(4,128)}, f32[4,1024]{1,0:T(4,128)}) all-reduce(f32[4,1024]{1,0:T(4,128)S(1)} %get-tuple-element.11, f32[4,1024]{1,0:T(4,128)S(1)} %get-tuple-element.7), channel_id=1, replica_groups=mesh['member'=2,'fsdp'=16] {'fsdp'}, use_global_device_ids=true, to_apply=%region_3.0 | all-reduce | flops 8192 | bytes 65536 | tf_op jit(solution)/shard_map/psum | solution.py:29
  216.5 31.5 %reduce-scatter.5.cloned.1.call-done = f32[128,1024]{1,0:T(8,128)} async-done(((f32[2048,1024]{1,0:T(8,128)}), f32[128,1024]{1,0:T(8,128)}) %reduce-scatter.5.cloned.1.call-update) | async-done | bytes 524304 | tf_op jit(solution)/shard_map/reduce_scatter | solution.py:33
  (2 shorter events, 0.0 us)
Async XLA Ops:
  7.2 56.1 %all-gather.5.cloned.1.call-start = ((), (), s32[]{:S(2)}) async-start(), calls=%async_computation.3 | async-start | bytes 4456448 | tf_op jit(solution)/shard_map/all_gather | solution.py:13
  7.9 92.2 %reduce-scatter.3.cloned.1.call-start = ((), (), s32[]{:S(2)}) async-start(), calls=%async_computation.4 | async-start | bytes 3145728 | tf_op jit(solution)/shard_map/reduce_scatter | solution.py:23
  69.5 0.7 copy-start.2
  69.5 30.6 %copy-start = (bf16[4,128,1024]{2,1,0:T(8,128)(2,1)S(1)}, bf16[4,128,1024]{2,1,0:T(8,128)(2,1)}, u32[]{:S(2)}) copy-start(bf16[4,128,1024]{2,1,0:T(8,128)(2,1)} %param.6) | copy-start | bytes 3145732
  69.5 67.1 %all-gather.3.cloned.1.call-start = ((), (), s32[]{:S(2)}) async-start(), calls=%async_computation.2 | async-start | bytes 3145728 | tf_op jit(solution)/shard_map/all_gather | solution.py:12
  70.2 66.4 %copy-start.4 = (bf16[4,128,1024]{2,1,0:T(8,128)(2,1)S(1)}, bf16[4,128,1024]{2,1,0:T(8,128)(2,1)}, u32[]{:S(2)}) copy-start(bf16[4,128,1024]{2,1,0:T(8,128)(2,1)} %param.11) | copy-start | bytes 3145732
  103.3 144.7 %reduce-scatter.5.cloned.1.call-start = ((), (), s32[]{:S(2)}) async-start(), calls=%async_computation.5 | async-start | bytes 8912896 | tf_op jit(solution)/shard_map/reduce_scatter | solution.py:33
  143.8 0.9 copy-start.1
  143.8 1.7 copy-start.3
Sparse Core Ops, SparseCore 0:
  10.1 53.0 all-gather.4
  69.6 30.4 reduce-scatter.2
  103.5 33.0 all-gather.2
  143.9 104.0 reduce-scatter.4
where the time goes:
time: 255 us
  waiting for transfers between devices  150 us (59%)
  blocking collectives  64.4 us (25%)
  matrix products  20 us (8%)
  between operations  13.8 us (5%)
  other arithmetic  3.96 us (2%)
    psum x1, blocking collectives, per_device(): grad_in, grad_out = lax.psum((grad_in_local, grad_out_local), 'fsdp')  64.4 us
    all_gather x1, waiting for transfers between devices, per_device(): weight = lax.all_gather(out_weight, 'fsdp', axis=0, tiled=True)  54.6 us
    all_gather x1, waiting for transfers between devices, per_device(): scaled_context = lax.all_gather(scaled_local, 'member', axis=2, tiled=True)  33.2 us
    reduce_scatter x1, waiting for transfers between devices, per_device(): lax.psum_scatter(grad_block, 'fsdp', scatter_dimension=0, tiled=True)  31.5 us
    reduce_scatter x1, waiting for transfers between devices, per_device(): lax.psum_scatter(partial_value.astype(jnp.bfloat16), 'member', scatter_di...  29.9 us
    dot_general x1, matrix products, per_device(): jnp.einsum('eti,etd->id', scaled_context, scaled_grad, preferred_element_...  7.2 us
    dot_general x1, matrix products, per_device(): jnp.einsum('eti,id->etd', scaled_context, weight, preferred_element_type=...  6.61 us
    dot_general x1, matrix products, per_device(): jnp.einsum('etd,id->eti', scaled_grad, weight, preferred_element_type=jnp...  6.22 us
  transfers between devices with their start and end apart: 4, of which 4 were waited for; matrix products, arithmetic and copies ran while one was open for 3% of the time, Pallas kernels for 0%

commit v1 on v0

--- a/solution.py
+++ b/solution.py
@@ -9,7 +9,8 @@
     out_wide = out_factor.astype(jnp.float32)
     scaled_local = (context.astype(jnp.float32) * in_wide[:, None, :]).astype(jnp.bfloat16)
     scaled_grad = (cotangent.astype(jnp.float32) * out_wide[:, None, :]).astype(jnp.bfloat16)
-    scaled_context = lax.all_gather(scaled_local, "member", axis=2, tiled=True)
+    parts = lax.all_gather(scaled_local, "member", axis=0, tiled=False)
+    scaled_context = jnp.concatenate(parts, axis=2)
     weight = lax.all_gather(out_weight, "fsdp", axis=0, tiled=True)
     projected = jnp.einsum(
         "eti,id->etd", scaled_context, weight, preferred_element_type=jnp.float32

time: 255 us -> 261 us (1.024)
  local copies, waits for them, and re-layouts: 2.24 us -> 8.81 us
    all_gather x0 -> x1, local copies, waits for them, and re-layouts: none -> 3.75 us  [per_device(): parts = lax.all_gather(scaled_local, 'member', axis=0, tiled=False)]
    reshape x0 -> x1, local copies, waits for them, and re-layouts: none -> 2.82 us  [per_device(): scaled_context = jnp.concatenate(parts, axis=2)]
where the time goes in v1:
time: 261 us
  waiting for transfers between devices  150 us (57%)
  blocking collectives  64.4 us (25%)
  matrix products  20 us (8%)
  between operations  13.8 us (5%)
  local copies, waits for them, and re-layouts  8.81 us (3%)
  other arithmetic  3.96 us (2%)
    psum x1, blocking collectives, per_device(): grad_in, grad_out = lax.psum((grad_in_local, grad_out_local), 'fsdp')  64.4 us
    all_gather x1, waiting for transfers between devices, per_device(): weight = lax.all_gather(out_weight, 'fsdp', axis=0, tiled=True)  54.6 us
    all_gather x1, waiting for transfers between devices, per_device(): parts = lax.all_gather(scaled_local, 'member', axis=0, tiled=False)  33.2 us
    reduce_scatter x1, waiting for transfers between devices, per_device(): lax.psum_scatter(grad_block, 'fsdp', scatter_dimension=0, tiled=True)  31.3 us
    reduce_scatter x1, waiting for transfers between devices, per_device(): lax.psum_scatter(partial_value.astype(jnp.bfloat16), 'member', scatter_di...  29.9 us
    dot_general x1, matrix products, per_device(): jnp.einsum('eti,etd->id', scaled_context, scaled_grad, preferred_element_...  7.2 us
    dot_general x1, matrix products, per_device(): jnp.einsum('eti,id->etd', scaled_context, weight, preferred_element_type=...  6.61 us
    dot_general x1, matrix products, per_device(): jnp.einsum('etd,id->eti', scaled_grad, weight, preferred_element_type=jnp...  6.22 us
  transfers between devices with their start and end apart: 4, of which 4 were waited for; matrix products, arithmetic and copies ran while one was open for 3% of the time, Pallas kernels for 0%

profile of v1, /device:TPU:0, one launch (start us, length us, event | category | flops | bytes accessed | tf_op | source)
XLA Modules:
  0.0 260.9 jit_solution(5874129493827920350)
XLA Ops:
  7.2 0.0 all-gather.4.cloned.1.call-start
  7.2 0.7 all-gather.4.cloned.1.call-update
  7.9 0.0 reduce-scatter.3.cloned.1.call-start
  7.9 0.7 convert_element_type.40
  8.6 54.6 %all-gather.4.cloned.1.call-done = bf16[2048,1024]{1,0:T(8,128)(2,1)} async-done(((bf16[128,1024]{1,0:T(8,128)(2,1)}), bf16[2048,1024]{1,0:T(8,128)(2,1)}) %all-gather.4.cloned.1.call-update) | async-done | bytes 4194320 | tf_op jit(solution)/shard_map/all_gather | solution.py:14
  63.3 6.2 %fusion.4 = bf16[4,128,2048]{2,1,0:T(8,128)(2,1)} fusion(bf16[2048,1024]{1,0:T(8,128)(2,1)} %all-gather.4.cloned.1.call-done, bf16[4,128,1024]{2,1,0:T(8,128)(2,1)} %param.11, f32[4,1024]{1,0:T(4,128)S(1)} %convert_element_type.40), kind=kOutput, calls=%fused_computation.8 | convolution fusion | flops 2150105088 | bytes 7356416 | tf_op jit(solution)/shard_map/etd,id->eti/dot_general | solution.py:18
  69.5 0.0 copy-start.3
  69.5 0.0 copy-start.1
  69.5 0.0 reduce-scatter.3.cloned.1.call-update
  69.5 0.0 all-gather.6.cloned.1.call-start
  69.6 0.6 copy-done.3
  70.2 29.9 %reduce-scatter.3.cloned.1.call-done = bf16[4,128,1024]{2,1,0:T(8,128)(2,1)} async-done(((bf16[4,128,2048]{2,1,0:T(8,128)(2,1)}), bf16[4,128,1024]{2,1,0:T(8,128)(2,1)}) %reduce-scatter.3.cloned.1.call-update) | async-done | bytes 1048592 | tf_op jit(solution)/shard_map/reduce_scatter | solution.py:24
  100.1 0.0 copy-done.1
  100.1 3.2 %fusion.9 = (f32[4,1024]{1,0:T(4,128)S(1)}, bf16[4,128,1024]{2,1,0:T(8,128)(2,1)}, bf16[4,128,1024]{2,1,0:T(8,128)(2,1)}) fusion(bf16[4,128,1024]{2,1,0:T(8,128)(2,1)} %reduce-scatter.3.cloned.1.call-done, bf16[4,128,1024]{2,1,0:T(8,128)(2,1)S(1)} %copy-done.1, f32[4,1024]{1,0:T(4,128)S(1)} %convert_element_type.38), kind=kLoop, calls=%fused_computation.14 | loop fusion | flops 4190208 | bytes 4227072 | tf_op jit(solution)/shard_map/reduce_sum | solution.py:28
  103.3 0.0 all-gather.6.cloned.1.call-update
  103.3 0.0 reduce-scatter.5.cloned.1.call-start
  103.4 33.2 %all-gather.6.cloned.1.call-done = bf16[8,128,1024]{2,1,0:T(8,128)(2,1)} async-done(((bf16[4,128,1024]{2,1,0:T(8,128)(2,1)}), bf16[8,128,1024]{2,1,0:T(8,128)(2,1)}) %all-gather.6.cloned.1.call-update) | async-done | bytes 2097168 | tf_op jit(solution)/shard_map/all_gather | solution.py:12
  136.6 3.7 %copy.18 = bf16[2,4,128,1024]{3,0,2,1:T(2,128)(2,1)S(1)} copy(bf16[2,4,128,1024]{3,2,1,0:T(8,128)(2,1)} %bitcast.18) | data formatting | bytes 4194304 | tf_op jit(solution)/shard_map/all_gather | solution.py:12
  140.3 0.0 copy-start.4
  140.4 2.8 %reshape.22 = bf16[4,128,2048]{2,1,0:T(8,128)(2,1)} reshape(bf16[4,128,2,1024]{3,2,1,0:T(2,128)(2,1)S(1)} %bitcast.17) | data formatting | bytes 4194304 | tf_op jit(solution)/shard_map/reshape | solution.py:13
  143.2 0.0 copy-done.4
  143.2 7.2 %convolution_bitcast_fusion = f32[2048,1024]{1,0:T(8,128)} fusion(bf16[4,128,2048]{2,1,0:T(8,128)(2,1)} %reshape.22, bf16[4,128,1024]{2,1,0:T(8,128)(2,1)S(1)} %copy-done.4, f32[4,1024]{1,0:T(4,128)S(1)} %convert_element_type.40), kind=kOutput, calls=%fused_computation | convolution fusion | flops 2149056512 | bytes 11550720 | tf_op jit(solution)/shard_map/eti,etd->id/dot_general | solution.py:31
  150.4 0.0 copy-start.2
  150.4 0.0 copy-start
  150.4 0.0 reduce-scatter.5.cloned.1.call-update
  150.4 0.9 copy-done.2
  151.4 0.7 copy-done
  152.1 6.6 %convert_reduce_fusion = (f32[128,1024]{1,0:T(8,128)}, f32[4,1024]{1,0:T(4,128)S(1)}, bf16[4,128,1024]{2,1,0:T(8,128)(2,1)}) fusion(bf16[4,128,1024]{2,1,0:T(8,128)(2,1)S(1)} %copy-done.4, f32[4,1024]{1,0:T(4,128)S(1)} %convert_element_type.40, f32[128,1024]{1,0:T(8,128)S(1)} %convert_element_type.36, bf16[4,128,2048]{2,1,0:T(8,128)(2,1)S(1)} %copy-done, ...), kind=kOutput, calls=%fused_computation.5 | convolution fusion | flops 2151018496 | bytes 9469952 | tf_op jit(solution)/shard_map/eti,id->etd/dot_general | solution.py:15
  158.7 64.4 %all-reduce = (f32[4,1024]{1,0:T(4,128)}, f32[4,1024]{1,0:T(4,128)}) all-reduce(f32[4,1024]{1,0:T(4,128)S(1)} %get-tuple-element.11, f32[4,1024]{1,0:T(4,128)S(1)} %get-tuple-element.7), channel_id=1, replica_groups=mesh['member'=2,'fsdp'=16] {'fsdp'}, use_global_device_ids=true, to_apply=%region_3.0 | all-reduce | flops 8192 | bytes 65536 | tf_op jit(solution)/shard_map/psum | solution.py:30
  223.1 31.3 %reduce-scatter.5.cloned.1.call-done = f32[128,1024]{1,0:T(8,128)} async-done(((f32[2048,1024]{1,0:T(8,128)}), f32[128,1024]{1,0:T(8,128)}) %reduce-scatter.5.cloned.1.call-update) | async-done | bytes 524304 | tf_op jit(solution)/shard_map/reduce_scatter | solution.py:34
  (2 shorter events, 0.0 us)
Async XLA Ops:
  7.2 56.1 %all-gather.4.cloned.1.call-start = ((), (), s32[]{:S(2)}) async-start(), calls=%async_computation.2 | async-start | bytes 4456448 | tf_op jit(solution)/shard_map/all_gather | solution.py:14
  7.9 92.2 %reduce-scatter.3.cloned.1.call-start = ((), (), s32[]{:S(2)}) async-start(), calls=%async_computation.3 | async-start | bytes 3145728 | tf_op jit(solution)/shard_map/reduce_scatter | solution.py:24
  69.5 0.7 copy-start.3
  69.5 30.6 %copy-start.1 = (bf16[4,128,1024]{2,1,0:T(8,128)(2,1)S(1)}, bf16[4,128,1024]{2,1,0:T(8,128)(2,1)}, u32[]{:S(2)}) copy-start(bf16[4,128,1024]{2,1,0:T(8,128)(2,1)} %param.6) | copy-start | bytes 3145732
  69.5 67.1 %all-gather.6.cloned.1.call-start = ((), (), s32[]{:S(2)}) async-start(), calls=%async_computation.5 | async-start | bytes 3145728 | tf_op jit(solution)/shard_map/all_gather | solution.py:12
  103.3 151.0 %reduce-scatter.5.cloned.1.call-start = ((), (), s32[]{:S(2)}) async-start(), calls=%async_computation.4 | async-start | bytes 8912896 | tf_op jit(solution)/shard_map/reduce_scatter | solution.py:34
  140.3 2.8 %copy-start.4 = (bf16[4,128,1024]{2,1,0:T(8,128)(2,1)S(1)}, bf16[4,128,1024]{2,1,0:T(8,128)(2,1)}, u32[]{:S(2)}) copy-start(bf16[4,128,1024]{2,1,0:T(8,128)(2,1)} %param.11) | copy-start | bytes 3145732
  150.4 0.9 copy-start.2
  150.4 1.7 copy-start
Sparse Core Ops, SparseCore 0:
  10.1 53.0 all-gather.3
  69.6 30.4 reduce-scatter.2
  103.5 33.0 all-gather.5
  150.5 103.7 reduce-scatter.4
